TPU v7x, 512 devices: a whole 4x4x16 slice. The times are simulated.
512 devices in a mesh: dp: 8 (over y, core), expert: 64 (over x, z).
Axes of the slice: x: 4, y: 4, z: 16, core: 2. Of those that a mesh axis runs over, the one named last changes fastest.
Arguments:
- tokens: bfloat16 [32768, 1024], P(('dp', 'expert')), may hold values from -6 to 6
- expert_ids: int32 [32768, 8], P(('dp', 'expert')), may hold values from 0 to 63, all different within a row; in each aligned block of 64 rows (0 to 63, 64 to 127, ...) at most 10 rows name the same one
- route_weight: float32 [32768, 8], P(('dp', 'expert')), may hold values from 0.05 to 0.5
- out_grad: bfloat16 [32768, 1024], P(('dp', 'expert')), may hold values from -6 to 6
- gate_weight: bfloat16 [64, 1024, 384], P('expert', 'dp'), may hold values from -0.1875 to 0.1875
- up_weight: bfloat16 [64, 1024, 384], P('expert', 'dp'), may hold values from -0.1875 to 0.1875
- down_weight: bfloat16 [64, 384, 1024], P('expert', None, 'dp'), may hold values from -0.3125 to 0.3125
Outputs:
- layer_out: bfloat16 [32768, 1024], P(('dp', 'expert'))
- token_grad: bfloat16 [32768, 1024], P(('dp', 'expert'))
- route_grad: float32 [32768, 8], P(('dp', 'expert'))
- gate_grad: float32 [64, 1024, 384], P('expert', 'dp')
- up_grad: float32 [64, 1024, 384], P('expert', 'dp')
- down_grad: float32 [64, 384, 1024], P('expert', None, 'dp')
Inputs may be any that keep to these rules, and one draw needn't show every extreme that they name: `expert_ids`: each token names 8 different experts. Among the 64 tokens of one device no expert is named by more than 10 tokens, and in every draw some expert is named by exactly 10 tokens of some device.
All inputs are finite; a program needn't handle non-finite values.
Results may differ from a plain program's by a relative error of at most 0.012.
Values may be sent and summed in bfloat16 or wider, within the bound.
No kernel may reach another device: no remote copies, remote signals or barrier semaphores. Data moves between devices by JAX's collectives and lax.ppermute only.
A program may use at most 64 MiB of HBM per device.

v0:
```python
import jax
import jax.numpy as jnp
from jax import lax
from jax.sharding import PartitionSpec as P


def layout(live_counts, slot_cap, padded_rows):
    owners = live_counts.shape[0]
    ends = jnp.cumsum(live_counts).astype(jnp.int32)
    starts = ends - live_counts
    total = ends[owners - 1]
    positions = jnp.arange(padded_rows, dtype=jnp.int32)
    source = jnp.minimum(
        jnp.sum((positions[:, None] >= ends[None, :]).astype(jnp.int32), 1), owners - 1
    )
    matches = source[:, None] == jnp.arange(owners, dtype=jnp.int32)[None, :]
    offset = positions - jnp.sum(jnp.where(matches, starts[None, :], 0), 1)
    valid = positions < total
    pick_rows = jnp.where(valid, source * slot_cap + offset, 0)
    slot_pos = jnp.arange(owners * slot_cap, dtype=jnp.int32) % slot_cap
    live_back = slot_pos < jnp.repeat(live_counts, slot_cap)
    back_rows = jnp.where(live_back, jnp.repeat(starts, slot_cap) + slot_pos, 0)
    return (pick_rows, valid, back_rows, live_back, total)


def compact(received, pick_rows, valid):
    feat_width = received.shape[2]
    rows = received.reshape(-1, feat_width)[pick_rows]
    return jnp.where(valid[:, None], rows, jnp.zeros_like(rows))


def spread(rows, back_rows, live_back, owners, slot_cap):
    picked = rows[back_rows]
    picked = jnp.where(live_back[:, None], picked, jnp.zeros_like(picked))
    return picked.reshape(owners, slot_cap, rows.shape[1])


def shards(tokens, expert_ids, route_weight, out_grad, gate_weight, up_weight, down_weight):
    block_rows = 128
    tok_rows, feat_width = tokens.shape
    top_picks = expert_ids.shape[1]
    hidden_units = gate_weight.shape[2]
    owners = lax.axis_size("expert")
    slot_cap = max(2, 5 * tok_rows * top_picks // (4 * owners))
    slot_total = owners * slot_cap
    padded_rows = -(-slot_total // block_rows) * block_rows
    flat_ids = expert_ids.reshape(-1)
    one_hot = (flat_ids[:, None] == jnp.arange(owners, dtype=jnp.int32)[None, :]).astype(jnp.int32)
    slot_rank = jnp.sum((jnp.cumsum(one_hot, 0) - one_hot) * one_hot, 1)
    pair_slots = flat_ids * slot_cap + slot_rank
    send_counts = jnp.sum(one_hot, 0).reshape(owners, 1)
    x_send = (
        jnp.zeros((slot_total, feat_width), jnp.bfloat16)
        .at[pair_slots]
        .set(jnp.repeat(tokens, top_picks, 0))
        .reshape(owners, slot_cap, feat_width)
    )
    pair_grad = (
        route_weight.reshape(-1, 1) * jnp.repeat(out_grad, top_picks, 0).astype(jnp.float32)
    ).astype(jnp.bfloat16)
    dy_send = (
        jnp.zeros((slot_total, feat_width), jnp.bfloat16)
        .at[pair_slots]
        .set(pair_grad)
        .reshape(owners, slot_cap, feat_width)
    )
    gate_full, up_full, down_full = (
        lax.all_gather(gate_weight, "dp", axis=1, tiled=True),
        lax.all_gather(up_weight, "dp", axis=1, tiled=True),
        lax.all_gather(down_weight, "dp", axis=2, tiled=True),
    )
    gate_full = gate_full[0]
    up_full = up_full[0]
    down_full = down_full[0]
    x_recv, recv_counts = (
        lax.all_to_all(x_send, "expert", split_axis=0, concat_axis=0, tiled=True),
        lax.all_to_all(send_counts, "expert", split_axis=0, concat_axis=0, tiled=True),
    )
    pick_rows, valid, back_rows, live_back, total = layout(recv_counts[:, 0], slot_cap, padded_rows)
    live_blocks = (total + block_rows - 1) // block_rows
    x_rows = compact(x_recv, pick_rows, valid)

    def forward_block(block_id, carry):
        y_buf, h_buf, g_buf, u_buf = carry
        row_start = block_id * block_rows
        x_blk = lax.dynamic_slice_in_dim(x_rows, row_start, block_rows, 0)
        gate_act = jnp.dot(x_blk, gate_full, preferred_element_type=jnp.float32)
        up_act = jnp.dot(x_blk, up_full, preferred_element_type=jnp.float32)
        hidden = (gate_act * jax.nn.sigmoid(gate_act) * up_act).astype(jnp.bfloat16)
        y_blk = jnp.dot(hidden, down_full, preferred_element_type=jnp.float32).astype(jnp.bfloat16)
        return (
            lax.dynamic_update_slice_in_dim(y_buf, y_blk, row_start, 0),
            lax.dynamic_update_slice_in_dim(h_buf, hidden, row_start, 0),
            lax.dynamic_update_slice_in_dim(g_buf, gate_act, row_start, 0),
            lax.dynamic_update_slice_in_dim(u_buf, up_act, row_start, 0),
        )

    forward_init = (
        jnp.zeros((padded_rows, feat_width), jnp.bfloat16),
        jnp.zeros((padded_rows, hidden_units), jnp.bfloat16),
        jnp.zeros((padded_rows, hidden_units), jnp.float32),
        jnp.zeros((padded_rows, hidden_units), jnp.float32),
    )
    y_rows, h_rows, g_rows, u_rows = lax.fori_loop(0, live_blocks, forward_block, forward_init)
    y_back = lax.all_to_all(
        spread(y_rows, back_rows, live_back, owners, slot_cap),
        "expert",
        split_axis=0,
        concat_axis=0,
        tiled=True,
    )
    dy_recv = lax.all_to_all(dy_send, "expert", split_axis=0, concat_axis=0, tiled=True)
    dy_rows = compact(dy_recv, pick_rows, valid)
    contract_last = (((1,), (1,)), ((), ()))
    contract_rows = (((0,), (0,)), ((), ()))

    def backward_block(block_id, carry):
        dx_buf, act_buf = carry
        row_start = block_id * block_rows
        dy_blk = lax.dynamic_slice_in_dim(dy_rows, row_start, block_rows, 0)
        gate_act = lax.dynamic_slice_in_dim(g_rows, row_start, block_rows, 0)
        up_act = lax.dynamic_slice_in_dim(u_rows, row_start, block_rows, 0)
        sigmoid_g = jax.nn.sigmoid(gate_act)
        hidden_grad = lax.dot_general(
            dy_blk, down_full, contract_last, preferred_element_type=jnp.float32
        )
        gate_back = (
            hidden_grad * up_act * sigmoid_g * (1.0 + gate_act * (1.0 - sigmoid_g))
        ).astype(jnp.bfloat16)
        up_back = (hidden_grad * gate_act * sigmoid_g).astype(jnp.bfloat16)
        dx_blk = (
            lax.dot_general(gate_back, gate_full, contract_last, preferred_element_type=jnp.float32)
            + lax.dot_general(up_back, up_full, contract_last, preferred_element_type=jnp.float32)
        ).astype(jnp.bfloat16)
        act_back = jnp.concatenate([gate_back, up_back], 1)
        return (
            lax.dynamic_update_slice_in_dim(dx_buf, dx_blk, row_start, 0),
            lax.dynamic_update_slice_in_dim(act_buf, act_back, row_start, 0),
        )

    backward_init = (
        jnp.zeros((padded_rows, feat_width), jnp.bfloat16),
        jnp.zeros((padded_rows, 2 * hidden_units), jnp.bfloat16),
    )
    dx_rows, act_rows = lax.fori_loop(0, live_blocks, backward_block, backward_init)
    grad_total = jnp.concatenate(
        [
            lax.dot_general(x_rows, act_rows, contract_rows, preferred_element_type=jnp.float32),
            lax.dot_general(dy_rows, h_rows, contract_rows, preferred_element_type=jnp.float32),
        ],
        1,
    )
    dx_back = lax.all_to_all(
        spread(dx_rows, back_rows, live_back, owners, slot_cap),
        "expert",
        split_axis=0,
        concat_axis=0,
        tiled=True,
    )
    y_pairs = y_back.reshape(-1, feat_width)[pair_slots].reshape(tok_rows, top_picks, feat_width)
    dx_pairs = dx_back.reshape(-1, feat_width)[pair_slots].reshape(tok_rows, top_picks, feat_width)
    layer_out = jnp.sum(route_weight[:, :, None] * y_pairs.astype(jnp.float32), 1).astype(
        jnp.bfloat16
    )
    route_grad = jnp.einsum("td,tkd->tk", out_grad, y_pairs, preferred_element_type=jnp.float32)
    token_grad = jnp.sum(dx_pairs.astype(jnp.float32), 1).astype(jnp.bfloat16)
    local_rows = feat_width // lax.axis_size("dp")
    summed = lax.psum(grad_total.astype(jnp.bfloat16), "dp").astype(jnp.float32)
    mine = lax.dynamic_slice_in_dim(summed, lax.axis_index("dp") * local_rows, local_rows, 0)
    gate_grad = mine[:, :hidden_units][None]
    up_grad = mine[:, hidden_units : 2 * hidden_units][None]
    down_grad = mine[:, 2 * hidden_units :].T[None]
    return (layer_out, token_grad, route_grad, gate_grad, up_grad, down_grad)


def solution(mesh):
    placed = (
        P(("dp", "expert"), None),
        P(("dp", "expert"), None),
        P(("dp", "expert"), None),
        P(("dp", "expert"), None),
        P("expert", "dp", None),
        P("expert", "dp", None),
        P("expert", None, "dp"),
    )
    return jax.shard_map(
        shards,
        mesh=mesh,
        in_specs=placed,
        out_specs=(
            P(("dp", "expert"), None),
            P(("dp", "expert"), None),
            P(("dp", "expert"), None),
            P("expert", "dp", None),
            P("expert", "dp", None),
            P("expert", None, "dp"),
        ),
        check_vma=False,
    )
```

profile of v0, /device:TPU:2, one launch (start us, length us, event | category | flops | bytes accessed | tf_op | source)
XLA Modules:
  0.0 552.6 jit_solution(12986864640239789348)
XLA Ops:
  10.6 18.6 %all-to-all-start = ((s32[64,1,1]{2,1,0:T(1,128)}), s32[64,1,1]{2,1,0:T(1,128)S(1)}, u32[]{:S(2)}, u32[]{:S(2)}) async-start(s32[64,1,1]{2,1,0:T(1,128)} %copy.48), calls=%async_computation | async-start | bytes 65536 | tf_op jit(solution)/shard_map/all_to_all | solution.py:77
  37.1 5.6 %all-to-all-done = s32[64,1,1]{2,1,0:T(1,128)S(1)} async-done(((s32[64,1,1]{2,1,0:T(1,128)}), s32[64,1,1]{2,1,0:T(1,128)S(1)}, u32[]{:S(2)}, u32[]{:S(2)}) %all-to-all-start) | async-done | bytes 288 | tf_op jit(solution)/shard_map/all_to_all | solution.py:77
  42.7 9.5 %all-to-all-start.3 = ((bf16[64,10,1024]{2,1,0:T(8,128)(2,1)}), bf16[64,10,1024]{2,1,0:T(8,128)(2,1)S(1)}, u32[]{:S(2)}, u32[]{:S(2)}) async-start(bf16[64,10,1024]{2,1,0:T(8,128)(2,1)} %reshape.248), calls=%async_computation.3 | async-start | bytes 4194304 | tf_op jit(solution)/shard_map/all_to_all | solution.py:112
  52.2 3.7 scatter_custom_fusion
  55.9 3.6 reshape.242
  59.5 90.4 %all-to-all-done.3 = bf16[64,10,1024]{2,1,0:T(8,128)(2,1)S(1)} async-done(((bf16[64,10,1024]{2,1,0:T(8,128)(2,1)}), bf16[64,10,1024]{2,1,0:T(8,128)(2,1)S(1)}, u32[]{:S(2)}, u32[]{:S(2)}) %all-to-all-start.3) | async-done | bytes 1310752 | tf_op jit(solution)/shard_map/all_to_all | solution.py:112
  149.9 7.5 %all-to-all-start.1 = ((bf16[64,10,1024]{2,1,0:T(8,128)(2,1)}), bf16[64,10,1024]{2,1,0:T(8,128)(2,1)}, u32[]{:S(2)}, u32[]{:S(2)}) async-start(bf16[64,10,1024]{2,1,0:T(8,128)(2,1)} %reshape.242), calls=%async_computation.1 | async-start | bytes 4194304 | tf_op jit(solution)/shard_map/all_to_all | solution.py:76
  157.5 13.9 %all_gather.9 = bf16[1,1024,384]{2,1,0:T(8,128)(2,1)S(1)} all-gather(bf16[1,128,384]{2,1,0:T(8,128)(2,1)S(1)} %copy-done.13), channel_id=1, replica_groups=mesh['dp'=8,'expert'=64] {'dp'}, dimensions={1}, use_global_device_ids=true | all-gather | bytes 884736 | tf_op jit(solution)/shard_map/all_gather | solution.py:68
  171.4 13.4 %all_gather.10 = bf16[1,1024,384]{2,1,0:T(8,128)(2,1)S(1)} all-gather(bf16[1,128,384]{2,1,0:T(8,128)(2,1)S(1)} %copy-done.14), channel_id=1, replica_groups=mesh['dp'=8,'expert'=64] {'dp'}, dimensions={1}, use_global_device_ids=true | all-gather | bytes 884736 | tf_op jit(solution)/shard_map/all_gather | solution.py:69
  184.8 14.1 %all_gather.11 = bf16[1,384,1024]{2,1,0:T(8,128)(2,1)} all-gather(bf16[1,384,128]{2,1,0:T(8,128)(2,1)S(1)} %copy-done.15), channel_id=1, replica_groups=mesh['dp'=8,'expert'=64] {'dp'}, dimensions={2}, use_global_device_ids=true | all-gather | bytes 884736 | tf_op jit(solution)/shard_map/all_gather | solution.py:70
  206.2 3.5 gather_fusion.3
  209.7 45.1 %all-to-all-done.1 = bf16[64,10,1024]{2,1,0:T(8,128)(2,1)} async-done(((bf16[64,10,1024]{2,1,0:T(8,128)(2,1)}), bf16[64,10,1024]{2,1,0:T(8,128)(2,1)}, u32[]{:S(2)}, u32[]{:S(2)}) %all-to-all-start.1) | async-done | bytes 1310752 | tf_op jit(solution)/shard_map/all_to_all | solution.py:76
  257.4 3.5 gather_fusion
  260.9 3.5 broadcast_select_fusion.2
  266.6 17.2 %while.28 = (s32[]{:T(128)}, bf16[640,1024]{1,0:T(8,128)(2,1)S(1)}, bf16[640,384]{1,0:T(8,128)(2,1)S(1)}, f32[640,384]{1,0:T(8,128)}, f32[640,384]{1,0:T(8,128)}...) while((s32[]{:T(128)}, bf16[640,1024]{1,0:T(8,128)(2,1)S(1)}, ...), condition=%wide.region_9.10_spmd, body=%wide.region_8.9_spmd.sunk | while | flops 302415872 | bytes 7768279 | solution.py:104
  286.1 13.1 %while.29 = (s32[]{:T(128)}, bf16[640,1024]{1,0:T(8,128)(2,1)S(1)}, bf16[640,768]{1,0:T(8,128)(2,1)}, s32[]{:T(128)}, bf16[640,1024]{1,0:T(8,128)(2,1)}, /*index...) while((s32[]{:T(128)}, bf16[640,1024]{1,0:T(8,128)(2,1)S(1)}, ...), condition=%wide.region_13.14_spmd, body=%wide.region_12.13_spmd.sunk | while | flops 303284224 | bytes 8258775 | solution.py:145
  299.1 3.5 gather_fusion.4
  302.6 3.6 gather.28
  306.2 3.5 gather_fusion.1
  309.7 3.7 gather.24
  313.5 3.3 broadcast_select_fusion
  316.7 112.2 %all_to_all.32 = bf16[64,10,1024]{2,1,0:T(8,128)(2,1)} all-to-all(bf16[64,10,1024]{2,1,0:T(8,128)(2,1)S(1)} %get-tuple-element.204), channel_id=1, replica_groups=mesh['dp'=8,'expert'=64] {'expert'}, dimensions={0} | all-to-all | bytes 2621440 | tf_op jit(solution)/shard_map/all_to_all | solution.py:153
  429.0 9.0 %all-to-all-start.2 = ((bf16[64,10,1024]{2,1,0:T(8,128)(2,1)}), bf16[64,10,1024]{2,1,0:T(8,128)(2,1)}, u32[]{:S(2)}, u32[]{:S(2)}) async-start(bf16[64,10,1024]{2,1,0:T(8,128)(2,1)} %get-tuple-element.205), calls=%async_computation.2 | async-start | bytes 4194304 | tf_op jit(solution)/shard_map/all_to_all | solution.py:105
  444.0 85.1 %all-reduce.2.cloned.1.call-done = bf16[1024,1152]{0,1:T(8,128)(2,1)} async-done(((bf16[1024,1152]{0,1:T(8,128)(2,1)}), bf16[1024,1152]{0,1:T(8,128)(2,1)}) %all-reduce.2.cloned.1.call-update) | async-done | bytes 2359312 | tf_op jit(solution)/shard_map/psum | solution.py:168
  (140 shorter events, 77.5 us)
Async XLA Ops:
  7.2 45.0 %copy-start = (bf16[64,1024]{1,0:T(8,128)(2,1)S(1)}, bf16[64,1024]{1,0:T(8,128)(2,1)}, u32[]{:S(2)}) copy-start(bf16[64,1024]{1,0:T(8,128)(2,1)} %param.11) | copy-start | bytes 393220
  10.6 32.1 %all-to-all-start = ((s32[64,1,1]{2,1,0:T(1,128)}), s32[64,1,1]{2,1,0:T(1,128)S(1)}, u32[]{:S(2)}, u32[]{:S(2)}) async-start(s32[64,1,1]{2,1,0:T(1,128)} %copy.48), calls=%async_computation | async-start | bytes 65536 | tf_op jit(solution)/shard_map/all_to_all | solution.py:77
  42.7 107.2 %all-to-all-start.3 = ((bf16[64,10,1024]{2,1,0:T(8,128)(2,1)}), bf16[64,10,1024]{2,1,0:T(8,128)(2,1)S(1)}, u32[]{:S(2)}, u32[]{:S(2)}) async-start(bf16[64,10,1024]{2,1,0:T(8,128)(2,1)} %reshape.248), calls=%async_computation.3 | async-start | bytes 4194304 | tf_op jit(solution)/shard_map/all_to_all | solution.py:112
  59.5 98.0 %copy-start.13 = (bf16[1,128,384]{2,1,0:T(8,128)(2,1)S(1)}, bf16[1,128,384]{2,1,0:T(8,128)(2,1)}, u32[]{:S(2)}) copy-start(bf16[1,128,384]{2,1,0:T(8,128)(2,1)} %param.15) | copy-start | bytes 294916
  59.5 111.9 %copy-start.14 = (bf16[1,128,384]{2,1,0:T(8,128)(2,1)S(1)}, bf16[1,128,384]{2,1,0:T(8,128)(2,1)}, u32[]{:S(2)}) copy-start(bf16[1,128,384]{2,1,0:T(8,128)(2,1)} %param.16) | copy-start | bytes 294916
  149.9 7.6 %copy-start.5 = (bf16[64,10,1024]{2,1,0:T(8,128)(2,1)}, bf16[64,10,1024]{2,1,0:T(8,128)(2,1)S(1)}, u32[]{:S(2)}) copy-start(bf16[64,10,1024]{2,1,0:T(8,128)(2,1)S(1)} %all-to-all-done.3) | copy-start | bytes 3932164
  149.9 104.9 %all-to-all-start.1 = ((bf16[64,10,1024]{2,1,0:T(8,128)(2,1)}), bf16[64,10,1024]{2,1,0:T(8,128)(2,1)}, u32[]{:S(2)}, u32[]{:S(2)}) async-start(bf16[64,10,1024]{2,1,0:T(8,128)(2,1)} %reshape.242), calls=%async_computation.1 | async-start | bytes 4194304 | tf_op jit(solution)/shard_map/all_to_all | solution.py:76
  157.4 27.3 %copy-start.15 = (bf16[1,384,128]{2,1,0:T(8,128)(2,1)S(1)}, bf16[1,384,128]{2,1,0:T(8,128)(2,1)}, u32[]{:S(2)}) copy-start(bf16[1,384,128]{2,1,0:T(8,128)(2,1)} %param.17) | copy-start | bytes 294916
  266.6 3.3 copy-start.3
  270.9 3.3 copy-start.3
  275.2 3.3 copy-start.3
  279.5 3.3 copy-start.3
  286.1 2.2 copy-start.2
  289.3 2.2 copy-start.2
  292.6 2.2 copy-start.2
  295.9 2.2 copy-start.2
  309.7 3.7 copy-start.4
  429.0 9.3 %copy-start.7 = (bf16[640,1024]{1,0:T(8,128)(2,1)S(1)}, bf16[640,1024]{1,0:T(8,128)(2,1)}, u32[]{:S(2)}) copy-start(bf16[640,1024]{1,0:T(8,128)(2,1)} %get-tuple-element.444) | copy-start | bytes 3932164
  429.0 9.3 %copy-start.9 = (bf16[640,384]{1,0:T(8,128)(2,1)S(1)}, bf16[640,384]{1,0:T(8,128)(2,1)}, u32[]{:S(2)}) copy-start(bf16[640,384]{1,0:T(8,128)(2,1)} %copy-done.8) | copy-start | bytes 1474564
  429.0 109.5 %all-to-all-start.2 = ((bf16[64,10,1024]{2,1,0:T(8,128)(2,1)}), bf16[64,10,1024]{2,1,0:T(8,128)(2,1)}, u32[]{:S(2)}, u32[]{:S(2)}) async-start(bf16[64,10,1024]{2,1,0:T(8,128)(2,1)} %get-tuple-element.205), calls=%async_computation.2 | async-start | bytes 4194304 | tf_op jit(solution)/shard_map/all_to_all | solution.py:105
  438.0 91.1 %all-reduce.2.cloned.1.call-start = ((), (), s32[]{:S(2)}) async-start(), calls=%async_computation.5 | async-start | bytes 4718592 | tf_op jit(solution)/shard_map/psum | solution.py:168
  438.3 1.3 copy-start.6
  541.0 2.1 copy-start.11
  541.0 3.4 copy-start.12
  (3 other events, 2.6 us)
Sparse Core Ops, SparseCore 0:
  444.1 84.9 all-reduce.1
where the time goes:
time: 554 us; the launch traced here: 553 us
  waiting for transfers between devices  226 us (41%)
  blocking collectives  154 us (28%)
  local copies, waits for them, and re-layouts  60 us (11%)
  starting transfers between devices  45 us (8%)
  matrix products  28.5 us (5%)
  other arithmetic  24 us (4%)
  between operations  15.1 us (3%)
    all_to_all x1, blocking collectives, shards(): lax.all_to_all(spread(dx_rows, back_rows, live_back, owners, slot_cap), '...  112 us
    all_to_all x1, waiting for transfers between devices, shards(): lax.all_to_all(dy_send, 'expert', split_axis=0, concat_axis=0, tiled=True)  90.4 us
    psum x1, waiting for transfers between devices, shards(): summed = lax.psum(grad_total.astype(jnp.bfloat16), 'dp').astype(jnp.float32)  85.1 us
    all_to_all x1, waiting for transfers between devices, shards(): lax.all_to_all(x_send, 'expert', split_axis=0, concat_axis=0, tiled=True)  45.1 us
    all_to_all x1, starting transfers between devices, shards(): lax.all_to_all(send_counts, 'expert', split_axis=0, concat_axis=0, tiled=...  18.6 us
    gather x4, local copies, waits for them, and re-layouts, spread(): picked = rows[back_rows]  14.3 us
    all_gather x1, blocking collectives, shards(): lax.all_gather(down_weight, 'dp', axis=2, tiled=True)  14.1 us
    all_gather x1, blocking collectives, shards(): lax.all_gather(gate_weight, 'dp', axis=1, tiled=True)  13.9 us
  transfers between devices with their start and end apart: 5, of which 4 were waited for; matrix products, arithmetic and copies ran while one was open for 7% of the time, Pallas kernels for 0%

commit v1 on v0

--- a/solution.py
+++ b/solution.py
@@ -165,7 +165,9 @@
     route_grad = jnp.einsum("td,tkd->tk", out_grad, y_pairs, preferred_element_type=jnp.float32)
     token_grad = jnp.sum(dx_pairs.astype(jnp.float32), 1).astype(jnp.bfloat16)
     local_rows = feat_width // lax.axis_size("dp")
-    summed = lax.psum(grad_total.astype(jnp.bfloat16), "dp").astype(jnp.float32)
+    summed = jnp.sum(lax.all_gather(grad_total.astype(jnp.bfloat16), "dp"), axis=0).astype(
+        jnp.float32
+    )
     mine = lax.dynamic_slice_in_dim(summed, lax.axis_index("dp") * local_rows, local_rows, 0)
     gate_grad = mine[:, :hidden_units][None]
     up_grad = mine[:, hidden_units : 2 * hidden_units][None]

time: 554 us -> 576 us (1.040)
  the two profiles are of different devices: /device:TPU:2 before, /device:TPU:38 now
where the time goes in v1:
time: 576 us; the launch traced here: 575 us
  waiting for transfers between devices  234 us (41%)
  blocking collectives  146 us (25%)
  local copies, waits for them, and re-layouts  61.1 us (11%)
  starting transfers between devices  44.2 us (8%)
  matrix products  39.1 us (7%)
  other arithmetic  35.4 us (6%)
  between operations  15.1 us (3%)
    all_to_all x1, blocking collectives, shards(): lax.all_to_all(spread(y_rows, back_rows, live_back, owners, slot_cap), 'e...  104 us
    all_to_all x1, waiting for transfers between devices, shards(): lax.all_to_all(spread(dx_rows, back_rows, live_back, owners, slot_cap), '...  92.6 us
    all_to_all x1, waiting for transfers between devices, shards(): lax.all_to_all(dy_send, 'expert', split_axis=0, concat_axis=0, tiled=True)  90.1 us
    all_to_all x1, waiting for transfers between devices, shards(): lax.all_to_all(x_send, 'expert', split_axis=0, concat_axis=0, tiled=True)  45.8 us
    all_to_all x1, starting transfers between devices, shards(): lax.all_to_all(send_counts, 'expert', split_axis=0, concat_axis=0, tiled=...  18.3 us
    all_gather x1, blocking collectives, shards(): lax.all_gather(down_weight, 'dp', axis=2, tiled=True)  14.8 us
    all_gather x1, blocking collectives, shards(): lax.all_gather(up_weight, 'dp', axis=1, tiled=True)  13.6 us
    all_gather x1, blocking collectives, shards(): lax.all_gather(gate_weight, 'dp', axis=1, tiled=True)  13.4 us
  transfers between devices with their start and end apart: 5, of which 4 were waited for; matrix products, arithmetic and copies ran while one was open for 9% of the time, Pallas kernels for 0%

profile of v1, /device:TPU:38, one launch (start us, length us, event | category | flops | bytes accessed | tf_op | source)
XLA Modules:
  0.0 574.9 jit_solution(8922200266470210533)
XLA Ops:
  10.6 18.3 %all-to-all-start = ((s32[64,1,1]{2,1,0:T(1,128)}), s32[64,1,1]{2,1,0:T(1,128)S(1)}, u32[]{:S(2)}, u32[]{:S(2)}) async-start(s32[64,1,1]{2,1,0:T(1,128)} %copy.49), calls=%async_computation | async-start | bytes 65536 | tf_op jit(solution)/shard_map/all_to_all | solution.py:77
  35.4 5.1 all-to-all-done
  40.5 10.0 %all-to-all-start.3 = ((bf16[64,10,1024]{2,1,0:T(8,128)(2,1)}), bf16[64,10,1024]{2,1,0:T(8,128)(2,1)S(1)}, u32[]{:S(2)}, u32[]{:S(2)}) async-start(bf16[64,10,1024]{2,1,0:T(8,128)(2,1)} %reshape.279), calls=%async_computation.3 | async-start | bytes 4194304 | tf_op jit(solution)/shard_map/all_to_all | solution.py:112
  50.6 3.7 scatter_custom_fusion
  54.3 3.6 reshape.273
  57.9 90.1 %all-to-all-done.3 = bf16[64,10,1024]{2,1,0:T(8,128)(2,1)S(1)} async-done(((bf16[64,10,1024]{2,1,0:T(8,128)(2,1)}), bf16[64,10,1024]{2,1,0:T(8,128)(2,1)S(1)}, u32[]{:S(2)}, u32[]{:S(2)}) %all-to-all-start.3) | async-done | bytes 1310752 | tf_op jit(solution)/shard_map/all_to_all | solution.py:112
  149.3 7.8 %all-to-all-start.1 = ((bf16[64,10,1024]{2,1,0:T(8,128)(2,1)}), bf16[64,10,1024]{2,1,0:T(8,128)(2,1)}, u32[]{:S(2)}, u32[]{:S(2)}) async-start(bf16[64,10,1024]{2,1,0:T(8,128)(2,1)} %reshape.273), calls=%async_computation.1 | async-start | bytes 4194304 | tf_op jit(solution)/shard_map/all_to_all | solution.py:76
  157.2 14.8 %all_gather.15 = bf16[1,384,1024]{2,1,0:T(8,128)(2,1)} all-gather(bf16[1,384,128]{2,1,0:T(8,128)(2,1)S(1)} %copy-done.9), channel_id=1, replica_groups=mesh['dp'=8,'expert'=64] {'dp'}, dimensions={2}, use_global_device_ids=true | all-gather | bytes 884736 | tf_op jit(solution)/shard_map/all_gather | solution.py:70
  172.0 13.4 %all_gather.13 = bf16[1,1024,384]{2,1,0:T(8,128)(2,1)S(1)} all-gather(bf16[1,128,384]{2,1,0:T(8,128)(2,1)S(1)} %copy-done.10), channel_id=1, replica_groups=mesh['dp'=8,'expert'=64] {'dp'}, dimensions={1}, use_global_device_ids=true | all-gather | bytes 884736 | tf_op jit(solution)/shard_map/all_gather | solution.py:68
  185.4 13.6 %all_gather.14 = bf16[1,1024,384]{2,1,0:T(8,128)(2,1)S(1)} all-gather(bf16[1,128,384]{2,1,0:T(8,128)(2,1)S(1)} %copy-done.11), channel_id=1, replica_groups=mesh['dp'=8,'expert'=64] {'dp'}, dimensions={1}, use_global_device_ids=true | all-gather | bytes 884736 | tf_op jit(solution)/shard_map/all_gather | solution.py:69
  205.7 3.5 gather_fusion.3
  209.2 45.8 %all-to-all-done.1 = bf16[64,10,1024]{2,1,0:T(8,128)(2,1)} async-done(((bf16[64,10,1024]{2,1,0:T(8,128)(2,1)}), bf16[64,10,1024]{2,1,0:T(8,128)(2,1)}, u32[]{:S(2)}, u32[]{:S(2)}) %all-to-all-start.1) | async-done | bytes 1310752 | tf_op jit(solution)/shard_map/all_to_all | solution.py:76
  257.6 3.5 gather_fusion
  261.1 3.4 broadcast_select_fusion.2
  267.5 24.6 %while.28 = (s32[]{:T(128)}, bf16[640,1024]{1,0:T(8,128)(2,1)S(1)}, bf16[640,384]{1,0:T(8,128)(2,1)}, f32[640,384]{1,0:T(8,128)}, f32[640,384]{1,0:T(8,128)}, /*...) while((s32[]{:T(128)}, bf16[640,1024]{1,0:T(8,128)(2,1)S(1)}, ...), condition=%wide.region_9.10_spmd, body=%wide.region_8.9_spmd.sunk | while | flops 302415872 | bytes 7768287 | solution.py:104
  294.2 16.3 %while.29 = (s32[]{:T(128)}, bf16[640,1024]{1,0:T(8,128)(2,1)S(1)}, bf16[640,768]{1,0:T(8,128)(2,1)}, s32[]{:T(128)}, bf16[640,1024]{1,0:T(8,128)(2,1)}, /*index...) while((s32[]{:T(128)}, bf16[640,1024]{1,0:T(8,128)(2,1)S(1)}, ...), condition=%wide.region_13.14_spmd, body=%wide.region_12.13_spmd.sunk | while | flops 303284224 | bytes 8258783 | solution.py:145
  316.0 4.3 copy.55
  320.9 3.5 gather_fusion.4
  324.4 3.6 gather.28
  332.4 4.5 broadcast_select_fusion
  336.9 104.5 %all_to_all.32 = bf16[64,10,1024]{2,1,0:T(8,128)(2,1)} all-to-all(bf16[64,10,1024]{2,1,0:T(8,128)(2,1)S(1)} %get-tuple-element.180), channel_id=1, replica_groups=mesh['dp'=8,'expert'=64] {'expert'}, dimensions={0} | all-to-all | bytes 2621440 | tf_op jit(solution)/shard_map/all_to_all | solution.py:105
  441.4 8.0 %all-to-all-start.4 = ((bf16[64,10,1024]{2,1,0:T(8,128)(2,1)}), bf16[64,10,1024]{2,1,0:T(8,128)(2,1)S(1)}, u32[]{:S(2)}, u32[]{:S(2)}) async-start(bf16[64,10,1024]{2,1,0:T(8,128)(2,1)} %get-tuple-element.179), calls=%async_computation.4 | async-start | bytes 4194304 | tf_op jit(solution)/shard_map/all_to_all | solution.py:153
  454.8 92.6 %all-to-all-done.4 = bf16[64,10,1024]{2,1,0:T(8,128)(2,1)S(1)} async-done(((bf16[64,10,1024]{2,1,0:T(8,128)(2,1)}), bf16[64,10,1024]{2,1,0:T(8,128)(2,1)S(1)}, u32[]{:S(2)}, u32[]{:S(2)}) %all-to-all-start.4) | async-done | bytes 1310752 | tf_op jit(solution)/shard_map/all_to_all | solution.py:153
  554.9 10.4 %reduce_sum.81 = bf16[1024,1152]{1,0:T(8,128)(2,1)S(1)} reduce(bf16[8,1024,1152]{2,1,0:T(8,128)(2,1)} %all-gather.2.cloned.1.call-done, bf16[]{:T(256)} %constant.74.clone.1), dimensions={0}, to_apply=%region_15.16 | reduce | flops 8257536 | bytes 21233666 | tf_op jit(solution)/shard_map/reduce_sum | solution.py:168
  (151 shorter events, 91.6 us)
Async XLA Ops:
  7.2 43.4 %copy-start = (bf16[64,1024]{1,0:T(8,128)(2,1)S(1)}, bf16[64,1024]{1,0:T(8,128)(2,1)}, u32[]{:S(2)}) copy-start(bf16[64,1024]{1,0:T(8,128)(2,1)} %param.11) | copy-start | bytes 393220
  7.2 23.6 %copy-start.12 = (f32[64,8]{0,1:T(8,128)S(1)}, f32[64,8]{0,1:T(8,128)}, u32[]{:S(2)}) copy-start(f32[64,8]{0,1:T(8,128)} %param.13) | copy-start | bytes 6148
  10.6 30.0 %all-to-all-start = ((s32[64,1,1]{2,1,0:T(1,128)}), s32[64,1,1]{2,1,0:T(1,128)S(1)}, u32[]{:S(2)}, u32[]{:S(2)}) async-start(s32[64,1,1]{2,1,0:T(1,128)} %copy.49), calls=%async_computation | async-start | bytes 65536 | tf_op jit(solution)/shard_map/all_to_all | solution.py:77
  40.5 107.4 %all-to-all-start.3 = ((bf16[64,10,1024]{2,1,0:T(8,128)(2,1)}), bf16[64,10,1024]{2,1,0:T(8,128)(2,1)S(1)}, u32[]{:S(2)}, u32[]{:S(2)}) async-start(bf16[64,10,1024]{2,1,0:T(8,128)(2,1)} %reshape.279), calls=%async_computation.3 | async-start | bytes 4194304 | tf_op jit(solution)/shard_map/all_to_all | solution.py:112
  57.9 99.4 %copy-start.9 = (bf16[1,384,128]{2,1,0:T(8,128)(2,1)S(1)}, bf16[1,384,128]{2,1,0:T(8,128)(2,1)}, u32[]{:S(2)}) copy-start(bf16[1,384,128]{2,1,0:T(8,128)(2,1)} %param.17) | copy-start | bytes 294916
  57.9 114.1 %copy-start.10 = (bf16[1,128,384]{2,1,0:T(8,128)(2,1)S(1)}, bf16[1,128,384]{2,1,0:T(8,128)(2,1)}, u32[]{:S(2)}) copy-start(bf16[1,128,384]{2,1,0:T(8,128)(2,1)} %param.15) | copy-start | bytes 294916
  149.3 105.7 %all-to-all-start.1 = ((bf16[64,10,1024]{2,1,0:T(8,128)(2,1)}), bf16[64,10,1024]{2,1,0:T(8,128)(2,1)}, u32[]{:S(2)}, u32[]{:S(2)}) async-start(bf16[64,10,1024]{2,1,0:T(8,128)(2,1)} %reshape.273), calls=%async_computation.1 | async-start | bytes 4194304 | tf_op jit(solution)/shard_map/all_to_all | solution.py:76
  157.1 28.2 %copy-start.11 = (bf16[1,128,384]{2,1,0:T(8,128)(2,1)S(1)}, bf16[1,128,384]{2,1,0:T(8,128)(2,1)}, u32[]{:S(2)}) copy-start(bf16[1,128,384]{2,1,0:T(8,128)(2,1)} %param.16) | copy-start | bytes 294916
  157.2 397.8 %all-gather.2.cloned.1.call-start = ((), (), s32[]{:S(2)}) async-start(), calls=%async_computation.5 | async-start | bytes 21233664 | tf_op jit(solution)/shard_map/all_gather | solution.py:168
  267.5 3.9 copy-start.4
  272.4 3.9 copy-start.4
  277.3 3.9 copy-start.4
  282.3 3.9 copy-start.4
  287.2 3.9 copy-start.4
  294.2 2.2 copy-start.3
  297.4 2.2 copy-start.3
  300.7 2.2 copy-start.3
  304.0 2.2 copy-start.3
  307.3 2.2 copy-start.3
  310.5 2.4 copy-start.6
  310.5 2.4 copy-start.8
  441.4 106.0 %all-to-all-start.4 = ((bf16[64,10,1024]{2,1,0:T(8,128)(2,1)}), bf16[64,10,1024]{2,1,0:T(8,128)(2,1)S(1)}, u32[]{:S(2)}, u32[]{:S(2)}) async-start(bf16[64,10,1024]{2,1,0:T(8,128)(2,1)} %get-tuple-element.179), calls=%async_computation.4 | async-start | bytes 4194304 | tf_op jit(solution)/shard_map/all_to_all | solution.py:153
  547.9 2.1 copy-start.7
  565.4 2.6 copy-start.1
  (2 other events, 2.2 us)
Sparse Core Ops, SparseCore 0:
  320.5 94.4 all-gather.1
